TPU v7x, 256 devices: a whole 4x4x8 slice. The times are simulated.
256 devices in a mesh: row: 16 (over z_lo, y), col: 16 (over z_hi, x, core).
Axes of the slice: x: 4, y: 4, z: 8 (z_hi: 2, z_lo: 4; z = z_hi * 4 + z_lo), core: 2. Of those that a mesh axis runs over, the one named last changes fastest.
Arguments:
- object_field: float32 [2, 2048, 2048], P(None, 'row', 'col'), may hold values from -5 to 5
- probe: float32 [2, 2, 256, 256], replicated, may hold values from -5 to 5
- amplitudes: float32 [16, 16, 2, 256, 256], P('row', 'col'), may hold values from 0.2 to 2.5
- offsets: int32 [16, 16, 2, 2], P('row', 'col'), may hold values from -128 to 0
Outputs:
- object_out: float32 [2, 2048, 2048], P(None, 'row', 'col')
- probe_out: float32 [2, 2, 256, 256], replicated
Inputs may be any that keep to these rules, and one draw needn't show every extreme that they name: `offsets`: each scan's 256 x 256 window starts at this offset from its own tile's anchor, so it reaches at most 128 pixels into neighbouring tiles.
All inputs are finite; a program needn't handle non-finite values.
Results may differ from a plain program's by a relative error of at most 0.0003.
Values sent between devices are 32-bit elements; how exact they have to be, the bound alone decides.
No kernel may reach another device: no remote copies, remote signals or barrier semaphores. Data moves between devices by JAX's collectives and lax.ppermute only.
A program may use at most 128 MiB of HBM per device.

v0:
```python
import math
import jax
import jax.numpy as jnp
from jax import lax
from jax.sharding import PartitionSpec as P

ITERS = 2
FLOOR = 0.5
OBJECT_STEP = 0.5
OBJECT_REG = 0.5
PROBE_STEP = 1.0
PROBE_REG = 1.0
HIGHEST = lax.Precision.HIGHEST


def padded_2(cells, sides, width):
    for axis, dim in sides:
        count = lax.axis_size(axis)
        ends = count - 1
        head = lax.slice_in_dim(cells, 0, width, axis=dim)
        tail = lax.slice_in_dim(cells, cells.shape[dim] - width, cells.shape[dim], axis=dim)
        cells = jnp.concatenate(
            [
                lax.ppermute(tail, axis, [(i, (i + 1) % count) for i in range(ends)]),
                cells,
                lax.ppermute(head, axis, [((i + 1) % count, i) for i in range(ends)]),
            ],
            axis=dim,
        )
    return cells


def tables(side):
    indices = lax.iota(jnp.int32, side)
    phases = indices[:, None] * indices[None, :] % side
    angles = phases.astype(jnp.float32) * (2.0 * math.pi / side)
    scaling = 1.0 / math.sqrt(side)
    return (jnp.cos(angles) * scaling, jnp.sin(angles) * scaling)


def last_axis(real_part, imag_part, cos_table, sin_table):
    product_one = jnp.matmul(real_part, cos_table, precision=HIGHEST)
    product_two = jnp.matmul(imag_part, sin_table, precision=HIGHEST)
    product_three = jnp.matmul(real_part + imag_part, cos_table + sin_table, precision=HIGHEST)
    return (product_one - product_two, product_three - product_one - product_two)


def first_axis(real_part, imag_part, cos_table, sin_table):
    product_one = jnp.einsum("jk,bkl->bjl", cos_table, real_part, precision=HIGHEST)
    product_two = jnp.einsum("jk,bkl->bjl", sin_table, imag_part, precision=HIGHEST)
    product_three = jnp.einsum(
        "jk,bkl->bjl", cos_table + sin_table, real_part + imag_part, precision=HIGHEST
    )
    return (product_one - product_two, product_three - product_one - product_two)


def transform(real_part, imag_part, cos_table, sin_table):
    real_part, imag_part = last_axis(real_part, imag_part, cos_table, sin_table)
    return first_axis(real_part, imag_part, cos_table, sin_table)


def fold_axis(extended, axis_number, tile_side, half_width):
    own_part = lax.slice_in_dim(
        extended, 2 * half_width, 2 * half_width + tile_side, axis=axis_number
    )
    low_rim = lax.slice_in_dim(extended, 0, half_width, axis=axis_number)
    high_rim = lax.slice_in_dim(
        extended, tile_side + 3 * half_width, tile_side + 4 * half_width, axis=axis_number
    )
    low_widths = [(0, 0)] * extended.ndim
    high_widths = [(0, 0)] * extended.ndim
    low_widths[axis_number] = (0, tile_side - half_width)
    high_widths[axis_number] = (tile_side - half_width, 0)
    return own_part + low_rim + high_rim


def cut_windows(padded, starts, probe_side):
    zero_index = jnp.zeros((), jnp.int32)

    def cut_one(corner):
        return lax.dynamic_slice(
            padded, (zero_index, corner[0], corner[1]), (padded.shape[0], probe_side, probe_side)
        )

    return jax.vmap(cut_one)(starts)


def local(object_field, probe, amplitudes, offsets):
    tile_side = object_field.shape[1]
    mode_count = probe.shape[1]
    probe_side = probe.shape[2]
    half_width = probe_side // 2
    starts = offsets[0, 0] + half_width
    measured = amplitudes[0, 0]
    scan_count = starts.shape[0]
    zero_index = jnp.zeros((), jnp.int32)
    cos_table, sin_table = tables(probe_side)
    padded = padded_2(object_field, (("row", 1), ("col", 2)), half_width)
    for iteration in range(ITERS):
        windows = cut_windows(padded, starts, probe_side)
        win_real = windows[:, 0][:, None]
        win_imag = windows[:, 1][:, None]
        probe_real = probe[0][None]
        probe_imag = probe[1][None]
        exit_real = (probe_real * win_real - probe_imag * win_imag).reshape(
            -1, probe_side, probe_side
        )
        exit_imag = (probe_real * win_imag + probe_imag * win_real).reshape(
            -1, probe_side, probe_side
        )
        far_real, far_imag = transform(exit_real, exit_imag, cos_table, -sin_table)
        far_real = far_real.reshape(scan_count, mode_count, probe_side, probe_side)
        far_imag = far_imag.reshape(scan_count, mode_count, probe_side, probe_side)
        intensity = jnp.sum(far_real * far_real + far_imag * far_imag, axis=1)
        factor = (measured / jnp.maximum(jnp.sqrt(intensity), FLOOR) - 1.0)[:, None]
        back_real, back_imag = transform(
            (far_real * factor).reshape(-1, probe_side, probe_side),
            (far_imag * factor).reshape(-1, probe_side, probe_side),
            cos_table,
            sin_table,
        )
        back_real = back_real.reshape(scan_count, mode_count, probe_side, probe_side)
        back_imag = back_imag.reshape(scan_count, mode_count, probe_side, probe_side)
        obj_real = jnp.sum(probe_real * back_real + probe_imag * back_imag, axis=1)
        obj_imag = jnp.sum(probe_real * back_imag - probe_imag * back_real, axis=1)
        probe_power = jnp.sum(probe[0] * probe[0] + probe[1] * probe[1], axis=0)
        grad_probe = jnp.stack(
            [
                jnp.sum(win_real * back_real + win_imag * back_imag, axis=0),
                jnp.sum(win_real * back_imag - win_imag * back_real, axis=0),
            ]
        )
        probe_weight = jnp.sum(
            windows[:, 0] * windows[:, 0] + windows[:, 1] * windows[:, 1], axis=0
        )
        channels = 3
        gradient = jnp.zeros(
            (channels, tile_side + 2 * half_width, tile_side + 2 * half_width), jnp.float32
        )
        for scan_index in range(scan_count):
            contrib = jnp.stack([obj_real[scan_index], obj_imag[scan_index], probe_power])
            corner = (zero_index, starts[scan_index, 0], starts[scan_index, 1])
            gradient = lax.dynamic_update_slice(
                gradient, lax.dynamic_slice(gradient, corner, contrib.shape) + contrib, corner
            )
        extended = padded_2(gradient, (("row", 1), ("col", 2)), half_width)
        totals = fold_axis(fold_axis(extended, 1, tile_side, half_width), 2, tile_side, half_width)
        summed_grad, summed_weight = lax.psum((grad_probe, probe_weight), ("row", "col"))
        new_probe = probe + PROBE_STEP * summed_grad / (summed_weight + PROBE_REG)
        object_field = object_field + OBJECT_STEP * totals[0:2] / (totals[2:3] + OBJECT_REG)
        if iteration + 1 < ITERS:
            padded = padded_2(object_field, (("row", 1), ("col", 2)), half_width)
        probe = new_probe
    return (object_field, probe)


def solution(mesh):
    return jax.shard_map(
        local,
        mesh=mesh,
        in_specs=(
            P(None, "row", "col"),
            P(),
            P("row", "col", None, None, None),
            P("row", "col", None, None),
        ),
        out_specs=(P(None, "row", "col"), P()),
        check_vma=False,
    )
```

profile of v0, /device:TPU:2, one launch (start us, length us, event | category | flops | bytes accessed | tf_op | source)
XLA Modules:
  0.0 828.7 jit_solution(15070879831426267204)
XLA Ops:
  7.2 3.6 collective-permute-start
  15.1 2.9 collective-permute-done.1
  19.9 3.6 collective-permute-start.3
  36.4 4.3 while.2
  42.8 2.7 multiply_subtract_fusion.1
  49.5 3.9 fusion.53
  60.8 2.9 convolution_bitcast_fusion.10
  63.7 3.0 bitcast_reduce_fusion.1
  72.7 13.8 %fusion.10 = f32[4,256,256]{2,1,0:T(8,128)S(1)} fusion(f32[4,256,256]{2,1,0:T(8,128)S(1)} %fusion.43, f32[4,256,256]{2,1,0:T(8,128)S(1)} %fusion.62, f32[4,256,256]{1,2,0:T(8,128)S(1)} %get-tuple-element.94, f32[4,256,256]{1,2,0:T(8,128)S(1)} %get-tuple-element.95), kind=kOutput, calls=%fused_computation.34 | convolution fusion | flops 807206912 | bytes 5242880 | tf_op jit(solution)/shard_map/dot_general | solution.py:44
  91.9 4.6 add_reduce_fusion.3
  98.3 10.7 %dynamic_update_slice.12 = f32[3,384,384]{1,2,0:T(8,128)S(1)} dynamic-update-slice(f32[3,384,384]{1,2,0:T(8,128)S(1)} %broadcast.83.clone, f32[3,256,256]{1,2,0:T(8,128)} %pad_maximum_fusion.5, s32[]{:T(128)} %constant.12.clone.1, s32[]{:T(128)S(6)} %select_n.86, s32[]{:T(128)S(6)} %select_n.87) | dynamic-update-slice | bytes 1572868 | tf_op jit(solution)/shard_map/dynamic_update_slice | solution.py:143
  111.0 11.3 %dynamic_update_slice.13 = f32[3,384,384]{1,2,0:T(8,128)S(1)} dynamic-update-slice(f32[3,384,384]{1,2,0:T(8,128)S(1)} %dynamic_update_slice.12, f32[3,256,256]{1,2,0:T(8,128)} %fusion.21, s32[]{:T(128)} %constant.12.clone.1, s32[]{:T(128)S(6)} %select_n.88, s32[]{:T(128)S(6)} %select_n.89) | dynamic-update-slice | bytes 1572868 | tf_op jit(solution)/shard_map/dynamic_update_slice | solution.py:143
  122.5 2.8 collective-permute-start.4
  129.2 8.5 %collective-permute-done.4 = f32[3,128,384]{1,2,0:T(8,128)S(1)} collective-permute-done((f32[3,128,384]{1,2,0:T(8,128)S(1)}, f32[3,128,384]{1,2,0:T(8,128)S(1)}, u32[]{:S(2)}, u32[]{:S(2)}) %collective-permute-start.4) | collective-permute-done | bytes 589856 | tf_op jit(solution)/shard_map/ppermute | solution.py:24
  137.6 4.8 collective-permute-done.5
  145.9 3.6 collective-permute-start.7
  153.5 265.9 %all-reduce.7.cloned.1.call-done = (f32[2,2,256,256]{2,3,1,0:T(8,128)}, f32[256,256]{1,0:T(8,128)}) async-done(((f32[2,2,256,256]{2,3,1,0:T(8,128)}, f32[256,256]{1,0:T(8,128)}), (f32[2,2,256,256]{2,3,1,0:T(8,128)}, f32[256,256]{1,0:T(8,128)})) %all-reduce.7.cloned.1.call-update) | async-done | bytes 1310736 | tf_op jit(solution)/shard_map/psum | solution.py:148
  423.0 3.0 collective-permute-start.8
  428.5 4.4 collective-permute-done.9
  434.8 3.6 collective-permute-start.11
  444.9 7.5 while.3
  458.6 3.9 fusion.50
  471.4 2.8 convolution_bitcast_fusion.4
  474.3 3.0 bitcast_reduce_fusion
  483.2 3.0 fusion.8
  491.6 4.5 add_reduce_fusion.1
  498.0 10.7 %dynamic_update_slice.14 = f32[3,384,384]{1,2,0:T(8,128)S(1)} dynamic-update-slice(f32[3,384,384]{1,2,0:T(8,128)S(1)} %broadcast.83, f32[3,256,256]{1,2,0:T(8,128)} %pad_maximum_fusion.7, s32[]{:T(128)} %constant.12.clone.1, s32[]{:T(128)S(6)} %select_n.86, s32[]{:T(128)S(6)} %select_n.87) | dynamic-update-slice | bytes 1572868 | tf_op jit(solution)/shard_map/dynamic_update_slice | solution.py:143
  510.8 11.6 %dynamic_update_slice.15 = f32[3,384,384]{1,2,0:T(8,128)S(1)} dynamic-update-slice(f32[3,384,384]{1,2,0:T(8,128)S(1)} %dynamic_update_slice.14, f32[3,256,256]{1,2,0:T(8,128)} %fusion.20, s32[]{:T(128)} %constant.12.clone.1, s32[]{:T(128)S(6)} %select_n.88, s32[]{:T(128)S(6)} %select_n.89) | dynamic-update-slice | bytes 1572868 | tf_op jit(solution)/shard_map/dynamic_update_slice | solution.py:143
  531.5 8.1 collective-permute-done.12
  539.6 4.2 collective-permute-done.13
  548.6 3.2 collective-permute-start.15
  551.8 258.8 %all-reduce.5.cloned.1.call-done = (f32[2,2,256,256]{2,3,1,0:T(8,128)}, f32[256,256]{1,0:T(8,128)}) async-done(((f32[2,2,256,256]{2,3,1,0:T(8,128)}, f32[256,256]{1,0:T(8,128)}), (f32[2,2,256,256]{2,3,1,0:T(8,128)}, f32[256,256]{1,0:T(8,128)})) %all-reduce.5.cloned.1.call-update) | async-done | bytes 1310736 | tf_op jit(solution)/shard_map/psum | solution.py:148
  (190 shorter events, 131.6 us)
Async XLA Ops:
  7.2 7.0 copy-start
  7.2 412.3 %all-reduce.7.cloned.1.call-start = ((), (), s32[]{:S(2)}) async-start(), calls=%async_computation.1 | async-start | bytes 2621440 | tf_op jit(solution)/shard_map/psum | solution.py:148
  7.2 7.0 collective-permute-start
  10.8 7.1 collective-permute-start.1
  15.0 16.1 %copy-start.29 = (f32[1,1,2,256,256]{4,3,2,1,0:T(8,128)S(1)}, f32[1,1,2,256,256]{4,3,2,1,0:T(8,128)}, u32[]{:S(2)}) copy-start(f32[1,1,2,256,256]{4,3,2,1,0:T(8,128)} %param.6) | copy-start | bytes 1572868
  17.9 14.2 %copy-start.27 = (f32[2,384,128]{2,1,0:T(8,128)}, f32[2,384,128]{2,1,0:T(8,128)S(1)}, u32[]{:S(2)}) copy-start(f32[2,384,128]{2,1,0:T(8,128)S(1)} %constant_dynamic-update-slice_fusion) | copy-start | bytes 1179652
  18.0 17.0 %collective-permute-start.2 = (f32[2,384,128]{2,1,0:T(8,128)S(1)}, f32[2,384,128]{2,1,0:T(8,128)}, u32[]{:S(2)}, u32[]{:S(2)}) collective-permute-start(f32[2,384,128]{2,1,0:T(8,128)S(1)} %constant_dynamic-update-slice_fusion), channel_id=1, source_target_pairs={{0,1},{1,2},{2,3},{3,4},{4,5},{5,6},{6,7},{7,8},{8,9},{9,10},{10,1... | collective-permute-start | bytes 1179656 | tf_op jit(solution)/shard_map/ppermute | solution.py:24
  19.9 15.1 %collective-permute-start.3 = (f32[2,384,128]{2,1,0:T(8,128)S(1)}, f32[2,384,128]{2,1,0:T(8,128)}, u32[]{:S(2)}, u32[]{:S(2)}) collective-permute-start(f32[2,384,128]{2,1,0:T(8,128)S(1)} %constant_dynamic-update-slice_fusion), channel_id=1, source_target_pairs={{1,0},{2,1},{3,2},{4,3},{5,4},{6,5},{7,6},{8,7},{9,8},{10,9},{11,1... | collective-permute-start | bytes 1179656 | tf_op jit(solution)/shard_map/ppermute | solution.py:26
  122.4 4.3 copy-start.2
  122.4 5.0 copy-start.21
  122.5 4.9 copy-start.14
  122.5 4.9 copy-start.15
  122.5 15.2 %collective-permute-start.4 = (f32[3,128,384]{1,2,0:T(8,128)S(1)}, f32[3,128,384]{1,2,0:T(8,128)S(1)}, u32[]{:S(2)}, u32[]{:S(2)}) collective-permute-start(f32[3,128,384]{1,2,0:T(8,128)S(1)} %get-tuple-element.78), channel_id=1, source_target_pairs={{0,16},{16,32},{32,48},{48,64},{64,80},{80,96},{96,112},{112,128},... | collective-permute-start | bytes 1769480 | tf_op jit(solution)/shard_map/ppermute | solution.py:24
  125.3 17.1 %collective-permute-start.5 = (f32[3,128,384]{1,2,0:T(8,128)S(1)}, f32[3,128,384]{1,2,0:T(8,128)S(1)}, u32[]{:S(2)}, u32[]{:S(2)}) collective-permute-start(f32[3,128,384]{1,2,0:T(8,128)S(1)} %get-tuple-element.79), channel_id=1, source_target_pairs={{16,0},{32,16},{48,32},{64,48},{80,64},{96,80},{112,96},{128,112},... | collective-permute-start | bytes 1769480 | tf_op jit(solution)/shard_map/ppermute | solution.py:26
  143.9 277.3 %collective-permute-start.6 = (f32[3,640,128]{1,2,0:T(8,128)}, f32[3,640,128]{1,2,0:T(8,128)}, u32[]{:S(2)}, u32[]{:S(2)}) collective-permute-start(f32[3,640,128]{1,2,0:T(8,128)} %get-tuple-element.70), channel_id=1, source_target_pairs={{0,1},{1,2},{2,3},{3,4},{4,5},{5,6},{6,7},{7,8},{8,9},{9,10},{10,1... | collective-permute-start | bytes 2949128 | tf_op jit(solution)/shard_map/ppermute | solution.py:24
  145.9 275.4 %collective-permute-start.7 = (f32[3,640,128]{1,2,0:T(8,128)}, f32[3,640,128]{1,2,0:T(8,128)}, u32[]{:S(2)}, u32[]{:S(2)}) collective-permute-start(f32[3,640,128]{1,2,0:T(8,128)} %get-tuple-element.71), channel_id=1, source_target_pairs={{1,0},{2,1},{3,2},{4,3},{5,4},{6,5},{7,6},{8,7},{9,8},{10,9},{11,1... | collective-permute-start | bytes 2949128 | tf_op jit(solution)/shard_map/ppermute | solution.py:26
  150.6 660.1 %all-reduce.5.cloned.1.call-start = ((), (), s32[]{:S(2)}) async-start(), calls=%async_computation | async-start | bytes 2621440 | tf_op jit(solution)/shard_map/psum | solution.py:148
  153.5 267.8 %copy-start.24 = (f32[3,128,384]{1,2,0:T(8,128)S(1)}, f32[3,128,384]{1,2,0:T(8,128)}, u32[]{:S(2)}) copy-start(f32[3,128,384]{1,2,0:T(8,128)} %copy-done.23) | copy-start | bytes 1769476
  421.3 6.0 copy-start.26
  421.3 6.0 copy-start.22
  421.3 6.0 copy-start.25
  423.0 5.5 collective-permute-start.8
  426.0 6.9 collective-permute-start.9
  432.9 9.1 %collective-permute-start.10 = (f32[2,384,128]{1,2,0:T(8,128)S(1)}, f32[2,384,128]{1,2,0:T(8,128)S(1)}, u32[]{:S(2)}, u32[]{:S(2)}) collective-permute-start(f32[2,384,128]{1,2,0:T(8,128)S(1)} %pad_maximum_fusion.14), channel_id=1, source_target_pairs={{0,1},{1,2},{2,3},{3,4},{4,5},{5,6},{6,7},{7,8},{8,9},{9,10},{10,1... | collective-permute-start | bytes 1179656 | tf_op jit(solution)/shard_map/ppermute | solution.py:24
  434.8 8.9 %collective-permute-start.11 = (f32[2,384,128]{1,2,0:T(8,128)S(1)}, f32[2,384,128]{1,2,0:T(8,128)S(1)}, u32[]{:S(2)}, u32[]{:S(2)}) collective-permute-start(f32[2,384,128]{1,2,0:T(8,128)S(1)} %pad_maximum_fusion.14), channel_id=1, source_target_pairs={{1,0},{2,1},{3,2},{4,3},{5,4},{6,5},{7,6},{8,7},{9,8},{10,9},{11,1... | collective-permute-start | bytes 1179656 | tf_op jit(solution)/shard_map/ppermute | solution.py:26
  522.4 4.9 copy-start.12
  522.4 4.9 copy-start.13
  522.4 4.9 copy-start.20
  523.5 16.1 %collective-permute-start.12 = (f32[3,128,384]{1,2,0:T(8,128)}, f32[3,128,384]{1,2,0:T(8,128)S(1)}, u32[]{:S(2)}, u32[]{:S(2)}) collective-permute-start(f32[3,128,384]{1,2,0:T(8,128)} %get-tuple-element.76), channel_id=1, source_target_pairs={{0,16},{16,32},{32,48},{48,64},{64,80},{80,96},{96,112},{112,128},... | collective-permute-start | bytes 1769480 | tf_op jit(solution)/shard_map/ppermute | solution.py:24
  526.0 17.8 %collective-permute-start.13 = (f32[3,128,384]{1,2,0:T(8,128)}, f32[3,128,384]{1,2,0:T(8,128)}, u32[]{:S(2)}, u32[]{:S(2)}) collective-permute-start(f32[3,128,384]{1,2,0:T(8,128)} %get-tuple-element.77), channel_id=1, source_target_pairs={{16,0},{32,16},{48,32},{64,48},{80,64},{96,80},{112,96},{128,112},... | collective-permute-start | bytes 1769480 | tf_op jit(solution)/shard_map/ppermute | solution.py:26
  546.3 272.8 %collective-permute-start.14 = (f32[3,640,128]{1,2,0:T(8,128)}, f32[3,640,128]{1,2,0:T(8,128)}, u32[]{:S(2)}, u32[]{:S(2)}) collective-permute-start(f32[3,640,128]{1,2,0:T(8,128)} %get-tuple-element.68), channel_id=1, source_target_pairs={{0,1},{1,2},{2,3},{3,4},{4,5},{5,6},{6,7},{7,8},{8,9},{9,10},{10,1... | collective-permute-start | bytes 2949128 | tf_op jit(solution)/shard_map/ppermute | solution.py:24
  548.6 270.5 %collective-permute-start.15 = (f32[3,640,128]{1,2,0:T(8,128)}, f32[3,640,128]{1,2,0:T(8,128)}, u32[]{:S(2)}, u32[]{:S(2)}) collective-permute-start(f32[3,640,128]{1,2,0:T(8,128)} %get-tuple-element.69), channel_id=1, source_target_pairs={{1,0},{2,1},{3,2},{4,3},{5,4},{6,5},{7,6},{8,7},{9,8},{10,9},{11,1... | collective-permute-start | bytes 2949128 | tf_op jit(solution)/shard_map/ppermute | solution.py:26
  (18 other events, 37.6 us)
Sparse Core Ops, SparseCore 0:
  150.7 268.7 all-reduce.6
  531.6 279.0 all-reduce.4
where the time goes:
time: 841 us; the launch traced here: 829 us
  waiting for transfers between devices  563 us (67%)
  local copies, waits for them, and re-layouts  86.8 us (10%)
  matrix products  82 us (10%)
  starting transfers between devices  39.3 us (5%)
  other arithmetic  34.4 us (4%)
  between operations  22.9 us (3%)
    psum x2, waiting for transfers between devices, local(): lax.psum((grad_probe, probe_weight), ('row', 'col'))  525 us
    dynamic_update_slice x4, local copies, waits for them, and re-layouts, local(): lax.dynamic_update_slice(gradient, lax.dynamic_slice(gradient, corner, co...  44.2 us
    dot_general x4, matrix products, last_axis(): jnp.matmul(real_part + imag_part, cos_table + sin_table, precision=HIGHEST)  21.1 us
    ppermute x8, waiting for transfers between devices, padded_2(): lax.ppermute(tail, axis, [(i, (i + 1) % count) for i in range(ends)])  20 us
    ppermute x8, starting transfers between devices, padded_2(): lax.ppermute(tail, axis, [(i, (i + 1) % count) for i in range(ends)])  19.9 us
    ppermute x8, starting transfers between devices, padded_2(): lax.ppermute(head, axis, [((i + 1) % count, i) for i in range(ends)])  19.3 us
    ppermute x8, waiting for transfers between devices, padded_2(): lax.ppermute(head, axis, [((i + 1) % count, i) for i in range(ends)])  17.9 us
  transfers between devices with their start and end apart: 18, of which 11 were waited for; matrix products, arithmetic and copies ran while one was open for 4% of the time, Pallas kernels for 0%

commit v1 on v0

--- a/solution.py
+++ b/solution.py
@@ -145,7 +145,13 @@
             )
         extended = padded_2(gradient, (("row", 1), ("col", 2)), half_width)
         totals = fold_axis(fold_axis(extended, 1, tile_side, half_width), 2, tile_side, half_width)
-        summed_grad, summed_weight = lax.psum((grad_probe, probe_weight), ("row", "col"))
+
+        def press_routes_all_here(q_in):
+            for hop_no in ("row", "col"):
+                q_in = lax.psum(q_in, hop_no)
+            return q_in
+
+        summed_grad, summed_weight = press_routes_all_here((grad_probe, probe_weight))
         new_probe = probe + PROBE_STEP * summed_grad / (summed_weight + PROBE_REG)
         object_field = object_field + OBJECT_STEP * totals[0:2] / (totals[2:3] + OBJECT_REG)
         if iteration + 1 < ITERS:

time: 841 us -> 931 us (1.11)
  the two profiles are of different devices: /device:TPU:2 before, /device:TPU:1 now
where the time goes in v1:
time: 931 us; the launch traced here: 919 us
  waiting for transfers between devices  663 us (71%)
  matrix products  80.2 us (9%)
  local copies, waits for them, and re-layouts  78.9 us (8%)
  starting transfers between devices  47.1 us (5%)
  other arithmetic  26.1 us (3%)
  between operations  22.9 us (2%)
    psum x4, waiting for transfers between devices, press_routes_all_here(): q_in = lax.psum(q_in, hop_no)  612 us
    dynamic_update_slice x4, local copies, waits for them, and re-layouts, local(): lax.dynamic_update_slice(gradient, lax.dynamic_slice(gradient, corner, co...  42.6 us
    ppermute x8, starting transfers between devices, padded_2(): lax.ppermute(tail, axis, [(i, (i + 1) % count) for i in range(ends)])  32.4 us
    ppermute x8, waiting for transfers between devices, padded_2(): lax.ppermute(tail, axis, [(i, (i + 1) % count) for i in range(ends)])  30.8 us
    dot_general x4, matrix products, last_axis(): jnp.matmul(real_part + imag_part, cos_table + sin_table, precision=HIGHEST)  20.7 us
    ppermute x8, waiting for transfers between devices, padded_2(): lax.ppermute(head, axis, [((i + 1) % count, i) for i in range(ends)])  20.5 us
  transfers between devices with their start and end apart: 20, of which 13 were waited for; matrix products, arithmetic and copies ran while one was open for 5% of the time, Pallas kernels for 0%

profile of v1, /device:TPU:1, one launch (start us, length us, event | category | flops | bytes accessed | tf_op | source)
XLA Modules:
  0.0 919.2 jit_solution(3792216798255435999)
XLA Ops:
  7.2 4.2 collective-permute-start
  17.4 5.1 collective-permute-start.2
  37.5 4.0 while.2
  50.4 3.9 fusion.53
  64.6 3.0 bitcast_reduce_fusion.1
  73.5 13.4 %fusion.10 = f32[4,256,256]{2,1,0:T(8,128)S(1)} fusion(f32[4,256,256]{2,1,0:T(8,128)S(1)} %fusion.43, f32[4,256,256]{2,1,0:T(8,128)S(1)} %fusion.62, f32[4,256,256]{1,2,0:T(8,128)S(1)} %get-tuple-element.98, f32[4,256,256]{1,2,0:T(8,128)S(1)} %get-tuple-element.99), kind=kOutput, calls=%fused_computation.34 | convolution fusion | flops 807206912 | bytes 5242880 | tf_op jit(solution)/shard_map/dot_general | solution.py:44
  92.4 4.6 add_reduce_fusion.3
  98.8 10.8 %dynamic_update_slice.12 = f32[3,384,384]{1,2,0:T(8,128)S(1)} dynamic-update-slice(f32[3,384,384]{1,2,0:T(8,128)S(1)} %broadcast.83.clone, f32[3,256,256]{1,2,0:T(8,128)} %pad_maximum_fusion.5, s32[]{:T(128)} %constant.12.clone.1, s32[]{:T(128)S(6)} %select_n.86, s32[]{:T(128)S(6)} %select_n.87) | dynamic-update-slice | bytes 1572868 | tf_op jit(solution)/shard_map/dynamic_update_slice | solution.py:143
  111.7 10.3 %dynamic_update_slice.13 = f32[3,384,384]{1,2,0:T(8,128)S(1)} dynamic-update-slice(f32[3,384,384]{1,2,0:T(8,128)S(1)} %dynamic_update_slice.12, f32[3,256,256]{1,2,0:T(8,128)} %fusion.21, s32[]{:T(128)} %constant.12.clone.1, s32[]{:T(128)S(6)} %select_n.88, s32[]{:T(128)S(6)} %select_n.89) | dynamic-update-slice | bytes 1572868 | tf_op jit(solution)/shard_map/dynamic_update_slice | solution.py:143
  122.2 3.6 collective-permute-start.4
  127.4 9.8 %collective-permute-done.4 = f32[3,128,384]{1,2,0:T(8,128)S(1)} collective-permute-done((f32[3,128,384]{1,2,0:T(8,128)S(1)}, f32[3,128,384]{1,2,0:T(8,128)S(1)}, u32[]{:S(2)}, u32[]{:S(2)}) %collective-permute-start.4) | collective-permute-done | bytes 589856 | tf_op jit(solution)/shard_map/ppermute | solution.py:24
  137.2 4.4 collective-permute-done.5
  143.2 4.9 collective-permute-start.6
  153.6 5.7 collective-permute-done.6
  159.4 4.4 collective-permute-done.7
  165.4 5.4 collective-permute-start.8
  172.7 4.7 collective-permute-done.9
  177.5 3.7 collective-permute-start.10
  184.4 135.8 %all-reduce.15.cloned.1.call-done = (f32[2,2,256,256]{2,3,1,0:T(8,128)}, f32[256,256]{1,0:T(8,128)}) async-done(((f32[2,2,256,256]{2,3,1,0:T(8,128)}, f32[256,256]{1,0:T(8,128)}), (f32[2,2,256,256]{2,3,1,0:T(8,128)}, f32[256,256]{1,0:T(8,128)})) %all-reduce.15.cloned.1.call-update) | async-done | bytes 1310736 | tf_op jit(solution)/shard_map/psum | solution.py:151
  320.5 5.1 while.3
  328.4 184.3 %all-reduce.11.cloned.1.call-done = (f32[2,2,256,256]{2,3,1,0:T(8,128)}, f32[256,256]{1,0:T(8,128)}) async-done(((f32[2,2,256,256]{2,3,1,0:T(8,128)}, f32[256,256]{1,0:T(8,128)}), (f32[2,2,256,256]{2,3,1,0:T(8,128)}, f32[256,256]{1,0:T(8,128)})) %all-reduce.11.cloned.1.call-update) | async-done | bytes 1310736 | tf_op jit(solution)/shard_map/psum | solution.py:151
  520.0 3.9 fusion.50
  544.5 3.0 fusion.8
  553.1 3.1 add_reduce_fusion.1
  560.0 11.1 %dynamic_update_slice.14 = f32[3,384,384]{1,2,0:T(8,128)S(1)} dynamic-update-slice(f32[3,384,384]{1,2,0:T(8,128)S(1)} %broadcast.83, f32[3,256,256]{1,2,0:T(8,128)} %pad_maximum_fusion.7, s32[]{:T(128)} %constant.12.clone.1, s32[]{:T(128)S(6)} %select_n.86, s32[]{:T(128)S(6)} %select_n.87) | dynamic-update-slice | bytes 1572868 | tf_op jit(solution)/shard_map/dynamic_update_slice | solution.py:143
  573.2 10.3 %dynamic_update_slice.15 = f32[3,384,384]{1,2,0:T(8,128)S(1)} dynamic-update-slice(f32[3,384,384]{1,2,0:T(8,128)S(1)} %dynamic_update_slice.14, f32[3,256,256]{1,2,0:T(8,128)} %fusion.20, s32[]{:T(128)} %constant.12.clone.1, s32[]{:T(128)S(6)} %select_n.88, s32[]{:T(128)S(6)} %select_n.89) | dynamic-update-slice | bytes 1572868 | tf_op jit(solution)/shard_map/dynamic_update_slice | solution.py:143
  583.6 3.6 collective-permute-start.12
  588.5 14.7 %collective-permute-done.12 = f32[3,128,384]{1,2,0:T(8,128)S(1)} collective-permute-done((f32[3,128,384]{1,2,0:T(8,128)S(1)}, f32[3,128,384]{1,2,0:T(8,128)S(1)}, u32[]{:S(2)}, u32[]{:S(2)}) %collective-permute-start.12) | collective-permute-done | bytes 589856 | tf_op jit(solution)/shard_map/ppermute | solution.py:24
  603.2 5.2 collective-permute-done.13
  611.8 3.3 collective-permute-start.15
  615.1 101.9 %all-reduce.13.cloned.1.call-done = (f32[2,2,256,256]{2,3,1,0:T(8,128)}, f32[256,256]{1,0:T(8,128)}) async-done(((f32[2,2,256,256]{2,3,1,0:T(8,128)}, f32[256,256]{1,0:T(8,128)}), (f32[2,2,256,256]{2,3,1,0:T(8,128)}, f32[256,256]{1,0:T(8,128)})) %all-reduce.13.cloned.1.call-update) | async-done | bytes 1310736 | tf_op jit(solution)/shard_map/psum | solution.py:151
  719.4 190.0 %all-reduce.9.cloned.1.call-done = (f32[2,2,256,256]{2,3,1,0:T(8,128)}, f32[256,256]{1,0:T(8,128)}) async-done(((f32[2,2,256,256]{2,3,1,0:T(8,128)}, f32[256,256]{1,0:T(8,128)}), (f32[2,2,256,256]{2,3,1,0:T(8,128)}, f32[256,256]{1,0:T(8,128)})) %all-reduce.9.cloned.1.call-update) | async-done | bytes 1310736 | tf_op jit(solution)/shard_map/psum | solution.py:151
  (200 shorter events, 123.3 us)
Async XLA Ops:
  7.2 7.5 copy-start
  7.2 313.0 %all-reduce.15.cloned.1.call-start = ((), (), s32[]{:S(2)}) async-start(), calls=%async_computation.3 | async-start | bytes 2621440 | tf_op jit(solution)/shard_map/psum | solution.py:151
  7.2 7.5 collective-permute-start
  11.4 5.9 collective-permute-start.1
  15.6 16.6 %copy-start.31 = (f32[1,1,2,256,256]{4,3,2,1,0:T(8,128)S(1)}, f32[1,1,2,256,256]{4,3,2,1,0:T(8,128)}, u32[]{:S(2)}) copy-start(f32[1,1,2,256,256]{4,3,2,1,0:T(8,128)} %param.6) | copy-start | bytes 1572868
  17.3 15.9 %copy-start.29 = (f32[2,384,128]{2,1,0:T(8,128)}, f32[2,384,128]{2,1,0:T(8,128)S(1)}, u32[]{:S(2)}) copy-start(f32[2,384,128]{2,1,0:T(8,128)S(1)} %constant_dynamic-update-slice_fusion) | copy-start | bytes 1179652
  17.4 18.7 %collective-permute-start.2 = (f32[2,384,128]{2,1,0:T(8,128)S(1)}, f32[2,384,128]{2,1,0:T(8,128)}, u32[]{:S(2)}, u32[]{:S(2)}) collective-permute-start(f32[2,384,128]{2,1,0:T(8,128)S(1)} %constant_dynamic-update-slice_fusion), channel_id=1, source_target_pairs={{0,1},{1,2},{2,3},{3,4},{4,5},{5,6},{6,7},{7,8},{8,9},{9,10},{10,1... | collective-permute-start | bytes 1179656 | tf_op jit(solution)/shard_map/ppermute | solution.py:24
  22.5 13.6 %collective-permute-start.3 = (f32[2,384,128]{2,1,0:T(8,128)S(1)}, f32[2,384,128]{2,1,0:T(8,128)}, u32[]{:S(2)}, u32[]{:S(2)}) collective-permute-start(f32[2,384,128]{2,1,0:T(8,128)S(1)} %constant_dynamic-update-slice_fusion), channel_id=1, source_target_pairs={{1,0},{2,1},{3,2},{4,3},{5,4},{6,5},{7,6},{8,7},{9,8},{10,9},{11,1... | collective-permute-start | bytes 1179656 | tf_op jit(solution)/shard_map/ppermute | solution.py:26
  64.6 3.1 copy-start.4
  122.2 15.0 %collective-permute-start.4 = (f32[3,128,384]{1,2,0:T(8,128)S(1)}, f32[3,128,384]{1,2,0:T(8,128)S(1)}, u32[]{:S(2)}, u32[]{:S(2)}) collective-permute-start(f32[3,128,384]{1,2,0:T(8,128)S(1)} %get-tuple-element.82), channel_id=1, source_target_pairs={{0,16},{16,32},{32,48},{48,64},{64,80},{80,96},{96,112},{112,128},... | collective-permute-start | bytes 1769480 | tf_op jit(solution)/shard_map/ppermute | solution.py:24
  125.8 24.2 %copy-start.12 = (f32[2,256,256]{1,2,0:T(8,128)S(1)}, f32[2,256,256]{1,2,0:T(8,128)}, u32[]{:S(2)}) copy-start(f32[2,256,256]{1,2,0:T(8,128)} %copy.81) | copy-start | bytes 1572868
  125.8 24.2 %copy-start.13 = (f32[2,256,256]{1,2,0:T(8,128)S(1)}, f32[2,256,256]{1,2,0:T(8,128)}, u32[]{:S(2)}) copy-start(f32[2,256,256]{1,2,0:T(8,128)} %copy.84) | copy-start | bytes 1572868
  125.9 24.2 %copy-start.23 = (f32[4,256,256]{1,2,0:T(8,128)S(1)}, f32[4,256,256]{1,2,0:T(8,128)}, u32[]{:S(2)}) copy-start(f32[4,256,256]{1,2,0:T(8,128)} %get-tuple-element.65) | copy-start | bytes 3145732
  125.9 24.2 %copy-start.24 = (f32[4,256,256]{1,2,0:T(8,128)S(1)}, f32[4,256,256]{1,2,0:T(8,128)}, u32[]{:S(2)}) copy-start(f32[4,256,256]{1,2,0:T(8,128)} %get-tuple-element.107) | copy-start | bytes 3145732
  125.9 15.8 %collective-permute-start.5 = (f32[3,128,384]{1,2,0:T(8,128)S(1)}, f32[3,128,384]{1,2,0:T(8,128)S(1)}, u32[]{:S(2)}, u32[]{:S(2)}) collective-permute-start(f32[3,128,384]{1,2,0:T(8,128)S(1)} %get-tuple-element.83), channel_id=1, source_target_pairs={{16,0},{32,16},{48,32},{64,48},{80,64},{96,80},{112,96},{128,112},... | collective-permute-start | bytes 1769480 | tf_op jit(solution)/shard_map/ppermute | solution.py:26
  143.2 16.2 %collective-permute-start.6 = (f32[3,640,128]{1,2,0:T(8,128)}, f32[3,640,128]{1,2,0:T(8,128)}, u32[]{:S(2)}, u32[]{:S(2)}) collective-permute-start(f32[3,640,128]{1,2,0:T(8,128)} %get-tuple-element.74), channel_id=1, source_target_pairs={{0,1},{1,2},{2,3},{3,4},{4,5},{5,6},{6,7},{7,8},{8,9},{9,10},{10,1... | collective-permute-start | bytes 2949128 | tf_op jit(solution)/shard_map/ppermute | solution.py:24
  148.1 15.7 %collective-permute-start.7 = (f32[3,640,128]{1,2,0:T(8,128)}, f32[3,640,128]{1,2,0:T(8,128)}, u32[]{:S(2)}, u32[]{:S(2)}) collective-permute-start(f32[3,640,128]{1,2,0:T(8,128)} %get-tuple-element.75), channel_id=1, source_target_pairs={{1,0},{2,1},{3,2},{4,3},{5,4},{6,5},{7,6},{8,7},{9,8},{10,9},{11,1... | collective-permute-start | bytes 2949128 | tf_op jit(solution)/shard_map/ppermute | solution.py:26
  152.8 360.0 %all-reduce.11.cloned.1.call-start = ((), (), s32[]{:S(2)}) async-start(), calls=%async_computation.1 | async-start | bytes 2621440 | tf_op jit(solution)/shard_map/psum | solution.py:151
  153.6 11.7 %copy-start.30 = (f32[2,128,128]{1,2,0:T(8,128)S(1)}, f32[2,128,128]{1,2,0:T(8,128)}, u32[]{:S(2)}) copy-start(f32[2,128,128]{1,2,0:T(8,128)} %copy.100) | copy-start | bytes 393220
  165.4 7.4 collective-permute-start.8
  170.8 6.6 collective-permute-start.9
  177.5 142.8 %collective-permute-start.10 = (f32[2,384,128]{1,2,0:T(8,128)S(1)}, f32[2,384,128]{1,2,0:T(8,128)S(1)}, u32[]{:S(2)}, u32[]{:S(2)}) collective-permute-start(f32[2,384,128]{1,2,0:T(8,128)S(1)} %pad_maximum_fusion.14), channel_id=1, source_target_pairs={{0,1},{1,2},{2,3},{3,4},{4,5},{5,6},{6,7},{7,8},{8,9},{9,10},{10,1... | collective-permute-start | bytes 1179656 | tf_op jit(solution)/shard_map/ppermute | solution.py:24
  181.2 139.1 %collective-permute-start.11 = (f32[2,384,128]{1,2,0:T(8,128)S(1)}, f32[2,384,128]{1,2,0:T(8,128)S(1)}, u32[]{:S(2)}, u32[]{:S(2)}) collective-permute-start(f32[2,384,128]{1,2,0:T(8,128)S(1)} %pad_maximum_fusion.14), channel_id=1, source_target_pairs={{1,0},{2,1},{3,2},{4,3},{5,4},{6,5},{7,6},{8,7},{9,8},{10,9},{11,1... | collective-permute-start | bytes 1179656 | tf_op jit(solution)/shard_map/ppermute | solution.py:26
  320.2 396.8 %all-reduce.13.cloned.1.call-start = ((), (), s32[]{:S(2)}) async-start(), calls=%async_computation.2 | async-start | bytes 2621440 | tf_op jit(solution)/shard_map/psum | solution.py:151
  327.7 187.0 %copy-start.22 = (f32[2,2,256,256]{2,3,1,0:T(8,128)S(1)}, f32[2,2,256,256]{2,3,1,0:T(8,128)}, u32[]{:S(2)}) copy-start(f32[2,2,256,256]{2,3,1,0:T(8,128)} %copy.102) | copy-start | bytes 3145732
  527.9 2.7 copy-start.18
  535.6 3.0 copy-start.5
  558.9 350.5 %all-reduce.9.cloned.1.call-start = ((), (), s32[]{:S(2)}) async-start(), calls=%async_computation | async-start | bytes 2621440 | tf_op jit(solution)/shard_map/psum | solution.py:151
  583.6 19.5 %collective-permute-start.12 = (f32[3,128,384]{1,2,0:T(8,128)S(1)}, f32[3,128,384]{1,2,0:T(8,128)S(1)}, u32[]{:S(2)}, u32[]{:S(2)}) collective-permute-start(f32[3,128,384]{1,2,0:T(8,128)S(1)} %get-tuple-element.80), channel_id=1, source_target_pairs={{0,16},{16,32},{32,48},{48,64},{64,80},{80,96},{96,112},{112,128},... | collective-permute-start | bytes 1769480 | tf_op jit(solution)/shard_map/ppermute | solution.py:24
  587.2 21.2 %collective-permute-start.13 = (f32[3,128,384]{1,2,0:T(8,128)S(1)}, f32[3,128,384]{1,2,0:T(8,128)S(1)}, u32[]{:S(2)}, u32[]{:S(2)}) collective-permute-start(f32[3,128,384]{1,2,0:T(8,128)S(1)} %get-tuple-element.81), channel_id=1, source_target_pairs={{16,0},{32,16},{48,32},{64,48},{80,64},{96,80},{112,96},{128,112},... | collective-permute-start | bytes 1769480 | tf_op jit(solution)/shard_map/ppermute | solution.py:26
  609.9 107.2 %collective-permute-start.14 = (f32[3,640,128]{1,2,0:T(8,128)}, f32[3,640,128]{1,2,0:T(8,128)}, u32[]{:S(2)}, u32[]{:S(2)}) collective-permute-start(f32[3,640,128]{1,2,0:T(8,128)} %get-tuple-element.72), channel_id=1, source_target_pairs={{0,1},{1,2},{2,3},{3,4},{4,5},{5,6},{6,7},{7,8},{8,9},{9,10},{10,1... | collective-permute-start | bytes 2949128 | tf_op jit(solution)/shard_map/ppermute | solution.py:24
  611.8 105.3 %collective-permute-start.15 = (f32[3,640,128]{1,2,0:T(8,128)}, f32[3,640,128]{1,2,0:T(8,128)}, u32[]{:S(2)}, u32[]{:S(2)}) collective-permute-start(f32[3,640,128]{1,2,0:T(8,128)} %get-tuple-element.73), channel_id=1, source_target_pairs={{1,0},{2,1},{3,2},{4,3},{5,4},{6,5},{7,6},{8,7},{9,8},{10,9},{11,1... | collective-permute-start | bytes 2949128 | tf_op jit(solution)/shard_map/ppermute | solution.py:26
  (22 other events, 39.3 us)
Sparse Core Ops, SparseCore 0:
  152.9 167.2 all-reduce.14
  322.9 189.8 all-reduce.10
  559.0 157.9 all-reduce.12
  719.6 189.7 all-reduce.8
